TPU v7x, 32 devices: a whole 2x2x4 slice. The times are simulated.
32 devices in a mesh: dp: 4 (over z), mp: 8 (over y, x, core).
Axes of the slice: x: 2, y: 2, z: 4, core: 2. Of those that a mesh axis runs over, the one named last changes fastest.
Arguments:
- hidden_in: bfloat16 [64, 8192], P(None, 'dp'), may hold values from -25 to 25
- norm_gain: bfloat16 [8192], P('dp'), may hold values from 0.099609375 to 1.8984375
- w_query: bfloat16 [8192, 8192], P('dp', 'mp'), may hold values from -0.0625 to 0.0625
- w_keyval: bfloat16 [8192, 2048], P('dp', 'mp'), may hold values from -0.25 to 0.25
- w_out: bfloat16 [8192, 8192], P('mp', 'dp'), may hold values from -0.5 to 0.5
- cache_slots: bfloat16 [2, 64, 2, 8, 512, 128], P(None, ('dp', 'mp')), may hold values from -140 to 140
- lengths: int32 [64], replicated, may hold values from 1 to 512, 16384 in all
- positions: int32 [64], replicated, may hold values from 0 to 8191
- slot_order: int32 [64], replicated, may hold values from 0 to 63, each once
Outputs:
- result: bfloat16 [64, 8192], P(None, 'dp')
Inputs may be any that keep to these rules, and one draw needn't show every extreme that they name: `lengths`: every request has at least one valid cache position; the longest has 512. `slot_order`: each request's cache sits in exactly one slot.
All inputs are finite; a program needn't handle non-finite values.
Results may differ from a plain program's by a relative error of at most 0.035.
Values may be sent and summed in bfloat16 or wider, within the bound.
A program may use at most 128 MiB of HBM per device.

v0:
```python
import math
import jax
import jax.numpy as jnp
from jax import lax
from jax.sharding import PartitionSpec as P

LAYERS = 2
norm_eps = 1e-05
rope_base = 500000.0


def rotate(values, at_positions):
    half_dim = values.shape[-1] // 2
    index_row = jnp.arange(half_dim, dtype=jnp.float32)
    frequency = jnp.exp(index_row * (-2.0 * math.log(rope_base) / values.shape[-1]))
    angles = at_positions.astype(jnp.float32)[:, None, None] * frequency
    cosines = jnp.cos(angles)
    sine_rows = jnp.sin(angles)
    first_half = values[..., :half_dim]
    second_half = values[..., half_dim:]
    return jnp.concatenate(
        [
            first_half * cosines - second_half * sine_rows,
            second_half * cosines + first_half * sine_rows,
        ],
        axis=-1,
    )


def attend(queries, fresh_keys, fresh_values, key_rows, values, slot_lengths):
    score_scale = 1.0 / math.sqrt(queries.shape[-1])
    scores = (
        jnp.einsum("rkgd,rktd->rkgt", queries, key_rows, preferred_element_type=jnp.float32)
        * score_scale
    )
    own_score = (
        jnp.einsum("rkgd,rkd->rkg", queries, fresh_keys, preferred_element_type=jnp.float32)
        * score_scale
    )
    positions_row = lax.broadcasted_iota(jnp.int32, (1, 1, 1, key_rows.shape[2]), 3)
    valid_keys = positions_row < slot_lengths[:, None, None, None]
    scores = jnp.where(valid_keys, scores, -jnp.inf)
    highest = jnp.maximum(jnp.max(scores, axis=-1), own_score)
    weights = jnp.exp(scores - highest[..., None])
    own_weight = jnp.exp(own_score - highest)
    denominator = jnp.sum(weights, axis=-1) + own_weight
    rounded = weights.astype(jnp.bfloat16)
    own_rounded = lax.optimization_barrier(own_weight.astype(jnp.bfloat16)).astype(jnp.float32)
    summed = jnp.einsum("rkgt,rktd->rkgd", rounded, values, preferred_element_type=jnp.float32)
    summed = summed + own_rounded[..., None] * fresh_values.astype(jnp.float32)[:, :, None, :]
    return (summed / denominator[..., None]).astype(jnp.bfloat16)


def shards(
    hidden_in, norm_gain, w_query, w_keyval, w_out, cache_slots, lengths, positions, slot_order
):
    total_rows = hidden_in.shape[0]
    data_count = lax.axis_size("dp")
    model_count = lax.axis_size("mp")
    owned_rows = cache_slots.shape[1]
    key_heads = cache_slots.shape[3]
    head_dim = cache_slots.shape[5]
    query_cols = w_query.shape[1]
    head_count = query_cols * model_count // head_dim
    group_size = head_count // key_heads
    model_width = hidden_in.shape[1] * data_count
    half_width = key_heads * head_dim
    inverse = (
        jnp.zeros((total_rows,), jnp.int32)
        .at[slot_order]
        .set(jnp.arange(total_rows, dtype=jnp.int32))
    )
    device_index = lax.axis_index("dp") * model_count + lax.axis_index("mp")
    slot_lengths = lax.dynamic_slice_in_dim(
        jnp.take(lengths, slot_order), device_index * owned_rows, owned_rows
    )
    slot_positions = lax.dynamic_slice_in_dim(
        jnp.take(positions, slot_order), device_index * owned_rows, owned_rows
    )
    gain_float = norm_gain.astype(jnp.float32)
    current = jnp.take(hidden_in, slot_order, axis=0)
    for layer_index in range(LAYERS):
        floats = current.astype(jnp.float32)
        squares = jnp.sum(floats * floats, axis=1)
        scaled = (floats * gain_float).astype(jnp.bfloat16)
        partial_value = jnp.concatenate(
            [
                jnp.dot(scaled, w_query, preferred_element_type=jnp.float32),
                jnp.dot(scaled, w_keyval, preferred_element_type=jnp.float32),
            ],
            axis=1,
        )
        summed = lax.psum_scatter(partial_value, "dp", scatter_dimension=0, tiled=True)
        square_sum = lax.psum_scatter(squares, "dp", scatter_dimension=0, tiled=True)
        inverse_rms = lax.rsqrt(square_sum / model_width + norm_eps)
        projected = summed * inverse_rms[:, None]
        arrived = lax.all_to_all(projected, "mp", split_axis=0, concat_axis=1, tiled=True)
        arrived = arrived.reshape(owned_rows, model_count, projected.shape[1])
        query_part = arrived[:, :, :query_cols].reshape(owned_rows, head_count, head_dim)
        keyval_part = arrived[:, :, query_cols:].reshape(owned_rows, 2 * half_width)
        queries = (
            rotate(query_part, slot_positions)
            .astype(jnp.bfloat16)
            .reshape(owned_rows, key_heads, group_size, head_dim)
        )
        fresh_keys = rotate(
            keyval_part[:, :half_width].reshape(owned_rows, key_heads, head_dim), slot_positions
        ).astype(jnp.bfloat16)
        fresh_values = (
            keyval_part[:, half_width:]
            .reshape(owned_rows, key_heads, head_dim)
            .astype(jnp.bfloat16)
        )
        layer_cache = cache_slots[layer_index]
        attended = attend(
            queries, fresh_keys, fresh_values, layer_cache[:, 0], layer_cache[:, 1], slot_lengths
        )
        attended = attended.reshape(owned_rows, head_count * head_dim)
        returned = lax.all_to_all(attended, "mp", split_axis=1, concat_axis=0, tiled=True)
        partial_out = jnp.dot(
            lax.all_gather(returned, "dp", axis=0, tiled=True),
            w_out,
            preferred_element_type=jnp.float32,
        )
        totals = lax.psum(partial_out, "mp")
        current = (floats + totals).astype(jnp.bfloat16)
    return jnp.take(current, inverse, axis=0)


def solution(mesh):
    placed = (
        P(None, "dp"),
        P("dp"),
        P("dp", "mp"),
        P("dp", "mp"),
        P("mp", "dp"),
        P(None, ("dp", "mp"), None, None, None, None),
        P(),
        P(),
        P(),
    )
    return jax.shard_map(
        shards, mesh=mesh, in_specs=placed, out_specs=P(None, "dp"), check_vma=False
    )
```

profile of v0, /device:TPU:0, one launch (start us, length us, event | category | flops | bytes accessed | tf_op | source)
XLA Modules:
  0.0 262.7 jit_solution(91832775183974861)
XLA Ops:
  6.5 0.8 convert_element_type.90
  7.3 0.7 compare_select_fusion.1
  8.0 2.0 gather_fusion
  10.0 1.4 gather_fusion.2
  11.4 0.7 broadcast_select_fusion.2
  12.1 0.3 fusion.28
  12.4 3.1 %fusion.30 = f32[64,1024]{1,0:T(8,128)S(1)} fusion(bf16[2048,1024]{1,0:T(8,128)(2,1)} %param.15, f32[2048]{0:T(1024)S(1)} %convert_element_type.90, bf16[64,2048]{1,0:T(8,128)(2,1)S(1)} %gather_fusion, pred[64]{0:T(512)(128)(4,1)S(1)} %get-tuple-element.10), kind=kOutput, calls=%fused_computation.50 | convolution fusion | flops 268959744 | bytes 4726848 | tf_op jit(solution)/shard_map/dot_general | solution.py:88
  15.5 0.7 pad_maximum_fusion
  16.3 0.2 fusion.15
  16.5 5.9 %fusion.59 = (bf16[1,2,2,8,512,128]{5,4,3,2,1,0:T(8,128)(2,1)}, bf16[1,2,2,8,512,128]{5,4,3,2,1,0:T(8,128)(2,1)}) fusion(bf16[2,2,2,8,512,128]{5,4,3,2,1,0:T(8,128)(2,1)} %param.18), kind=kLoop, calls=%fused_computation.118 | loop fusion | bytes 16777216 | tf_op jit(solution)/shard_map/slice | solution.py:114
  22.4 13.4 %all-reduce = f32[64]{0:T(128)S(1)} all-reduce(f32[64]{0:T(128)S(1)} %fusion.15), channel_id=3, replica_groups=mesh['dp'=4,'mp'=8] {'dp'}, use_global_device_ids=true, to_apply=%region_2.0.clone | all-reduce | flops 64 | bytes 512
  35.8 0.8 gather_fusion.1
  36.6 0.6 dynamic-slice
  38.2 5.9 %copy_bitcast_fusion = (bf16[2,2,8,512,128]{4,3,2,0,1:T(8,128)(2,1)}, bf16[2,2,8,512,128]{4,3,2,0,1:T(8,128)(2,1)}) fusion(bf16[1,2,2,8,512,128]{5,4,3,2,1,0:T(8,128)(2,1)} %get-tuple-element.12, bf16[1,2,2,8,512,128]{5,4,3,2,1,0:T(8,128)(2,1)} %get-tuple-element.11), kind=kLoop, calls=%fused_computation.5 | loop fusion | bytes 16777216 | tf_op jit(solution)/shard_map/squeeze | solution.py:114
  44.2 1.0 broadcast_multiply_fusion.1
  45.1 0.7 all_to_all.52
  45.8 3.7 %all-to-all-start = ((f32[8,2,1280]{2,1,0:T(2,128)}), f32[8,2,1280]{2,1,0:T(2,128)S(1)}, u32[]{:S(2)}, u32[]{:S(2)}) async-start(f32[8,2,1280]{2,1,0:T(2,128)} %all_to_all.52), calls=%async_computation.1 | async-start | bytes 163840 | tf_op jit(solution)/shard_map/all_to_all | solution.py:97
  49.6 5.0 %all-to-all-done = f32[8,2,1280]{2,1,0:T(2,128)S(1)} async-done(((f32[8,2,1280]{2,1,0:T(2,128)}), f32[8,2,1280]{2,1,0:T(2,128)S(1)}, u32[]{:S(2)}, u32[]{:S(2)}) %all-to-all-start) | async-done | bytes 81952 | tf_op jit(solution)/shard_map/all_to_all | solution.py:97
  55.2 2.4 fusion.60
  57.8 2.0 fusion.13
  59.9 7.2 %all_to_all.70 = bf16[2,8,1024]{2,0,1:T(2,128)(2,1)S(1)} all-to-all(bf16[2,8,1024]{2,0,1:T(2,128)(2,1)S(1)} %copy.21), channel_id=1, replica_groups=mesh['dp'=4,'mp'=8] {'mp'}, dimensions={1} | all-to-all | bytes 65536 | tf_op jit(solution)/shard_map/all_to_all | solution.py:119
  67.2 13.5 %all_gather.6 = bf16[64,1024]{1,0:T(8,128)(2,1)S(1)} all-gather(bf16[16,1024]{1,0:T(8,128)(2,1)S(1)} %all_to_all.58), channel_id=1, replica_groups=mesh['dp'=4,'mp'=8] {'dp'}, dimensions={0}, use_global_device_ids=true | all-gather | bytes 163840 | tf_op jit(solution)/shard_map/all_gather | solution.py:121
  80.7 3.9 %fusion.62 = f32[64,2048]{1,0:T(8,128)} fusion(bf16[64,1024]{1,0:T(8,128)(2,1)S(1)} %all_gather.6, bf16[1024,2048]{1,0:T(8,128)(2,1)} %param.17), kind=kOutput, calls=%fused_computation.121 | convolution fusion | flops 268435456 | bytes 4849664 | tf_op jit(solution)/shard_map/dot_general | solution.py:120
  84.6 51.1 %all-reduce.5.cloned.1.call-done = f32[64,2048]{1,0:T(8,128)} async-done(((f32[64,2048]{1,0:T(8,128)}), f32[64,2048]{1,0:T(8,128)}) %all-reduce.5.cloned.1.call-update) | async-done | bytes 524304 | tf_op jit(solution)/shard_map/psum | solution.py:125
  135.7 1.3 fusion.18
  137.0 0.3 fusion.24
  137.3 3.0 %fusion.26 = f32[64,1024]{1,0:T(8,128)S(1)} fusion(bf16[2048,1024]{1,0:T(8,128)(2,1)} %param.15, bf16[64,2048]{1,0:T(8,128)(2,1)S(1)} %get-tuple-element.8, f32[2048]{0:T(1024)S(1)} %convert_element_type.90), kind=kOutput, calls=%fused_computation.48 | convolution fusion | flops 268828672 | bytes 4726784 | tf_op jit(solution)/shard_map/dot_general | solution.py:88
  140.3 0.7 pad_maximum_fusion.1
  141.1 11.7 %all-reduce.1 = f32[64]{0:T(128)S(1)} all-reduce(f32[64]{0:T(128)S(1)} %get-tuple-element.6), channel_id=5, replica_groups=mesh['dp'=4,'mp'=8] {'dp'}, use_global_device_ids=true, to_apply=%region_8.11.clone | all-reduce | flops 64 | bytes 512
  152.9 7.7 %reduce-scatter.5.cloned.1.call-done = f32[16,1280]{1,0:T(8,128)} async-done(((f32[64,1280]{1,0:T(8,128)}), f32[16,1280]{1,0:T(8,128)}) %reduce-scatter.5.cloned.1.call-update) | async-done | bytes 81936 | tf_op jit(solution)/shard_map/reduce_scatter | solution.py:93
  160.6 1.0 broadcast_multiply_fusion
  161.6 0.7 all_to_all.59
  162.3 3.7 %all-to-all-start.2 = ((f32[8,2,1280]{2,1,0:T(2,128)}), f32[8,2,1280]{2,1,0:T(2,128)S(1)}, u32[]{:S(2)}, u32[]{:S(2)}) async-start(f32[8,2,1280]{2,1,0:T(2,128)} %all_to_all.59), calls=%async_computation.4 | async-start | bytes 163840 | tf_op jit(solution)/shard_map/all_to_all | solution.py:97
  165.9 0.8 scatter_custom_fusion
  166.7 4.3 %all-to-all-done.2 = f32[8,2,1280]{2,1,0:T(2,128)S(1)} async-done(((f32[8,2,1280]{2,1,0:T(2,128)}), f32[8,2,1280]{2,1,0:T(2,128)S(1)}, u32[]{:S(2)}, u32[]{:S(2)}) %all-to-all-start.2) | async-done | bytes 81952 | tf_op jit(solution)/shard_map/all_to_all | solution.py:97
  171.4 2.4 fusion.61
  173.7 0.2 fusion.40
  174.0 0.2 fusion.22
  174.2 2.0 fusion.12
  176.3 0.6 copy.24
  176.9 3.3 %all-to-all-start.3 = ((bf16[2,8,1024]{2,0,1:T(2,128)(2,1)}), bf16[2,8,1024]{2,0,1:T(2,128)(2,1)S(1)}, u32[]{:S(2)}, u32[]{:S(2)}) async-start(bf16[2,8,1024]{2,0,1:T(2,128)(2,1)} %copy.24), calls=%async_computation.5 | async-start | bytes 65536 | tf_op jit(solution)/shard_map/all_to_all | solution.py:119
  180.3 4.7 %all-to-all-done.3 = bf16[2,8,1024]{2,0,1:T(2,128)(2,1)S(1)} async-done(((bf16[2,8,1024]{2,0,1:T(2,128)(2,1)}), bf16[2,8,1024]{2,0,1:T(2,128)(2,1)S(1)}, u32[]{:S(2)}, u32[]{:S(2)}) %all-to-all-start.3) | async-done | bytes 32800 | tf_op jit(solution)/shard_map/all_to_all | solution.py:119
  185.1 13.5 %all_gather.7 = bf16[64,1024]{1,0:T(8,128)(2,1)S(1)} all-gather(bf16[16,1024]{1,0:T(8,128)(2,1)S(1)} %all_to_all.65), channel_id=1, replica_groups=mesh['dp'=4,'mp'=8] {'dp'}, dimensions={0}, use_global_device_ids=true | all-gather | bytes 163840 | tf_op jit(solution)/shard_map/all_gather | solution.py:121
  198.6 3.8 %fusion.63 = f32[64,2048]{1,0:T(8,128)} fusion(bf16[64,1024]{1,0:T(8,128)(2,1)S(1)} %all_gather.7, bf16[1024,2048]{1,0:T(8,128)(2,1)} %param.17), kind=kOutput, calls=%fused_computation.122 | convolution fusion | flops 268435456 | bytes 4849664 | tf_op jit(solution)/shard_map/dot_general | solution.py:120
  202.5 51.1 %all-reduce.7.cloned.1.call-done = f32[64,2048]{1,0:T(8,128)} async-done(((f32[64,2048]{1,0:T(8,128)}), f32[64,2048]{1,0:T(8,128)}) %all-reduce.7.cloned.1.call-update) | async-done | bytes 524304 | tf_op jit(solution)/shard_map/psum | solution.py:125
  253.5 1.1 fusion.19
  254.6 0.7 gather_fusion.3
  255.4 0.8 broadcast_select_fusion
  (63 shorter events, 1.9 us)
Async XLA Ops:
  6.5 5.5 %copy-start = (bf16[2048,256]{1,0:T(8,128)(2,1)S(1)}, bf16[2048,256]{1,0:T(8,128)(2,1)}, u32[]{:S(2)}) copy-start(bf16[2048,256]{1,0:T(8,128)(2,1)} %param.16) | copy-start | bytes 3145732
  6.5 37.6 %reduce-scatter.3.cloned.1.call-start = ((), (), s32[]{:S(2)}) async-start(), calls=%async_computation.6 | async-start | bytes 409600 | tf_op jit(solution)/shard_map/reduce_scatter | solution.py:93
  16.5 19.3 %copy-start.1 = (s32[64]{0:T(128)S(1)}, s32[64]{0:T(128)}, u32[]{:S(2)}) copy-start(s32[64]{0:T(128)} %param.19) | copy-start | bytes 772
  16.5 20.1 %copy-start.2 = (u32[32]{0:T(128)S(1)}, u32[32]{0:T(128)}, u32[]{:S(2)}) copy-start(u32[32]{0:T(128)} %constant.56) | copy-start | bytes 388
  45.8 8.8 %all-to-all-start = ((f32[8,2,1280]{2,1,0:T(2,128)}), f32[8,2,1280]{2,1,0:T(2,128)S(1)}, u32[]{:S(2)}, u32[]{:S(2)}) async-start(f32[8,2,1280]{2,1,0:T(2,128)} %all_to_all.52), calls=%async_computation.1 | async-start | bytes 163840 | tf_op jit(solution)/shard_map/all_to_all | solution.py:97
  49.5 86.2 %all-reduce.5.cloned.1.call-start = ((), (), s32[]{:S(2)}) async-start(), calls=%async_computation.7 | async-start | bytes 1048576 | tf_op jit(solution)/shard_map/psum | solution.py:125
  84.5 76.1 %reduce-scatter.5.cloned.1.call-start = ((), (), s32[]{:S(2)}) async-start(), calls=%async_computation.8 | async-start | bytes 409600 | tf_op jit(solution)/shard_map/reduce_scatter | solution.py:93
  162.3 8.8 %all-to-all-start.2 = ((f32[8,2,1280]{2,1,0:T(2,128)}), f32[8,2,1280]{2,1,0:T(2,128)S(1)}, u32[]{:S(2)}, u32[]{:S(2)}) async-start(f32[8,2,1280]{2,1,0:T(2,128)} %all_to_all.59), calls=%async_computation.4 | async-start | bytes 163840 | tf_op jit(solution)/shard_map/all_to_all | solution.py:97
  176.9 8.1 %all-to-all-start.3 = ((bf16[2,8,1024]{2,0,1:T(2,128)(2,1)}), bf16[2,8,1024]{2,0,1:T(2,128)(2,1)S(1)}, u32[]{:S(2)}, u32[]{:S(2)}) async-start(bf16[2,8,1024]{2,0,1:T(2,128)(2,1)} %copy.24), calls=%async_computation.5 | async-start | bytes 65536 | tf_op jit(solution)/shard_map/all_to_all | solution.py:119
  180.3 73.2 %all-reduce.7.cloned.1.call-start = ((), (), s32[]{:S(2)}) async-start(), calls=%async_computation.9 | async-start | bytes 1048576 | tf_op jit(solution)/shard_map/psum | solution.py:125
Sparse Core Ops, SparseCore 0:
  16.4 22.8 reduce-scatter.2
  84.7 50.9 all-reduce.4
  141.2 19.3 reduce-scatter.4
  202.6 50.9 all-reduce.6
where the time goes:
time: 264 us; the launch traced here: 263 us
  waiting for transfers between devices  124 us (47%)
  blocking collectives  59.3 us (22%)
  matrix products  23.7 us (9%)
  local copies, waits for them, and re-layouts  20.5 us (8%)
  between operations  14.1 us (5%)
  starting transfers between devices  10.8 us (4%)
  other arithmetic  10.4 us (4%)
    psum x2, waiting for transfers between devices, shards(): totals = lax.psum(partial_out, 'mp')  102 us
    all_gather x2, blocking collectives, shards(): lax.all_gather(returned, 'dp', axis=0, tiled=True)  27 us
    unnamed x2, blocking collectives  25.1 us
    all_to_all x2, waiting for transfers between devices, shards(): lax.all_to_all(projected, 'mp', split_axis=0, concat_axis=1, tiled=True)  9.31 us
    reduce_scatter x2, waiting for transfers between devices, shards(): lax.psum_scatter(partial_value, 'dp', scatter_dimension=0, tiled=True)  7.74 us
    dot_general x2, matrix products, shards(): jnp.dot(lax.all_gather(returned, 'dp', axis=0, tiled=True), w_out, prefer...  7.69 us
    all_to_all x2, starting transfers between devices, shards(): lax.all_to_all(projected, 'mp', split_axis=0, concat_axis=1, tiled=True)  7.36 us
    all_to_all x1, blocking collectives, shards(): lax.all_to_all(attended, 'mp', split_axis=1, concat_axis=0, tiled=True)  7.22 us
  transfers between devices with their start and end apart: 7, of which 6 were waited for; matrix products, arithmetic and copies ran while one was open for 6% of the time, Pallas kernels for 0%

commit v1 on v0

--- a/solution.py
+++ b/solution.py
@@ -94,7 +94,12 @@
         square_sum = lax.psum_scatter(squares, "dp", scatter_dimension=0, tiled=True)
         inverse_rms = lax.rsqrt(square_sum / model_width + norm_eps)
         projected = summed * inverse_rms[:, None]
-        arrived = lax.all_to_all(projected, "mp", split_axis=0, concat_axis=1, tiled=True)
+        arrived = jnp.concatenate(
+            lax.all_to_all(
+                jnp.stack(jnp.split(projected, lax.axis_size("mp"), axis=0)), "mp", 0, 0
+            ),
+            axis=1,
+        )
         arrived = arrived.reshape(owned_rows, model_count, projected.shape[1])
         query_part = arrived[:, :, :query_cols].reshape(owned_rows, head_count, head_dim)
         keyval_part = arrived[:, :, query_cols:].reshape(owned_rows, 2 * half_width)

time: 264 us -> 272 us (1.030)
  local copies, waits for them, and re-layouts: 20.5 us -> 28.7 us
    unnamed x13 -> x27, local copies, waits for them, and re-layouts: 0.62 us -> 9.06 us
  transfers between devices with their start and end apart: 7 -> 7, of which waited for: 6 -> 6; matrix products, arithmetic and copies ran while one was open for 6% -> 5% of each run, Pallas kernels for 0% -> 0%
where the time goes in v1:
time: 272 us; the launch traced here: 271 us
  waiting for transfers between devices  124 us (46%)
  blocking collectives  59.5 us (22%)
  local copies, waits for them, and re-layouts  28.7 us (11%)
  matrix products  23.7 us (9%)
  between operations  14.1 us (5%)
  starting transfers between devices  10.8 us (4%)
  other arithmetic  10.4 us (4%)
    psum x2, waiting for transfers between devices, shards(): totals = lax.psum(partial_out, 'mp')  102 us
    all_gather x2, blocking collectives, shards(): lax.all_gather(returned, 'dp', axis=0, tiled=True)  27.2 us
    unnamed x2, blocking collectives  25.1 us
    all_to_all x2, waiting for transfers between devices, shards(): lax.all_to_all(jnp.stack(jnp.split(projected, lax.axis_size('mp'), axis=0...  9.31 us
    unnamed x27, local copies, waits for them, and re-layouts  9.06 us
    reduce_scatter x2, waiting for transfers between devices, shards(): lax.psum_scatter(partial_value, 'dp', scatter_dimension=0, tiled=True)  7.74 us
    dot_general x2, matrix products, shards(): jnp.dot(lax.all_gather(returned, 'dp', axis=0, tiled=True), w_out, prefer...  7.69 us
    all_to_all x2, starting transfers between devices, shards(): lax.all_to_all(jnp.stack(jnp.split(projected, lax.axis_size('mp'), axis=0...  7.36 us
  transfers between devices with their start and end apart: 7, of which 6 were waited for; matrix products, arithmetic and copies ran while one was open for 5% of the time, Pallas kernels for 0%

profile of v1, /device:TPU:0, one launch (start us, length us, event | category | flops | bytes accessed | tf_op | source)
XLA Modules:
  0.0 271.2 jit_solution(6451374794084236256)
XLA Ops:
  6.5 0.8 convert_element_type.90
  7.3 0.7 compare_select_fusion.1
  8.0 2.0 gather_fusion
  10.0 1.4 gather_fusion.2
  11.4 0.7 broadcast_select_fusion.2
  12.4 3.1 %fusion.30 = f32[64,1024]{1,0:T(8,128)S(1)} fusion(bf16[2048,1024]{1,0:T(8,128)(2,1)} %param.15, f32[2048]{0:T(1024)S(1)} %convert_element_type.90, bf16[64,2048]{1,0:T(8,128)(2,1)S(1)} %gather_fusion, pred[64]{0:T(512)(128)(4,1)S(1)} %get-tuple-element.10), kind=kOutput, calls=%fused_computation.50 | convolution fusion | flops 268959744 | bytes 4726848 | tf_op jit(solution)/shard_map/dot_general | solution.py:88
  15.5 0.7 pad_maximum_fusion
  16.5 5.9 %fusion.59 = (bf16[1,2,2,8,512,128]{5,4,3,2,1,0:T(8,128)(2,1)}, bf16[1,2,2,8,512,128]{5,4,3,2,1,0:T(8,128)(2,1)}) fusion(bf16[2,2,2,8,512,128]{5,4,3,2,1,0:T(8,128)(2,1)} %param.18), kind=kLoop, calls=%fused_computation.150 | loop fusion | bytes 16777216 | tf_op jit(solution)/shard_map/slice | solution.py:119
  22.4 13.4 %all-reduce = f32[64]{0:T(128)S(1)} all-reduce(f32[64]{0:T(128)S(1)} %fusion.15), channel_id=3, replica_groups=mesh['dp'=4,'mp'=8] {'dp'}, use_global_device_ids=true, to_apply=%region_2.0.clone | all-reduce | flops 64 | bytes 512
  35.8 0.8 gather_fusion.1
  38.2 5.9 %copy_bitcast_fusion = (bf16[2,2,8,512,128]{4,3,2,0,1:T(8,128)(2,1)}, bf16[2,2,8,512,128]{4,3,2,0,1:T(8,128)(2,1)}) fusion(bf16[1,2,2,8,512,128]{5,4,3,2,1,0:T(8,128)(2,1)} %get-tuple-element.12, bf16[1,2,2,8,512,128]{5,4,3,2,1,0:T(8,128)(2,1)} %get-tuple-element.11), kind=kLoop, calls=%fused_computation.5 | loop fusion | bytes 16777216 | tf_op jit(solution)/shard_map/squeeze | solution.py:119
  44.2 1.0 broadcast_multiply_fusion.1
  45.7 0.6 constant_dynamic-update-slice_fusion.6
  46.3 0.6 constant_dynamic-update-slice_fusion.5
  46.9 0.6 constant_dynamic-update-slice_fusion.4
  48.1 0.6 constant_dynamic-update-slice_fusion.2
  48.7 0.6 constant_dynamic-update-slice_fusion.1
  49.3 0.6 constant_dynamic-update-slice_fusion
  50.0 3.7 %all-to-all-start = ((f32[8,2,1280]{2,1,0:T(2,128)}), f32[8,2,1280]{2,1,0:T(2,128)S(1)}, u32[]{:S(2)}, u32[]{:S(2)}) async-start(f32[8,2,1280]{2,1,0:T(2,128)} %constant_dynamic-update-slice_fusion), calls=%async_computation.1 | async-start | bytes 163840 | tf_op jit(solution)/shard_map/all_to_all | solution.py:98
  53.8 5.0 %all-to-all-done = f32[8,2,1280]{2,1,0:T(2,128)S(1)} async-done(((f32[8,2,1280]{2,1,0:T(2,128)}), f32[8,2,1280]{2,1,0:T(2,128)S(1)}, u32[]{:S(2)}, u32[]{:S(2)}) %all-to-all-start) | async-done | bytes 81952 | tf_op jit(solution)/shard_map/all_to_all | solution.py:98
  59.3 2.4 fusion.60
  62.0 2.0 fusion.13
  64.1 7.2 %all_to_all.48 = bf16[2,8,1024]{2,0,1:T(2,128)(2,1)S(1)} all-to-all(bf16[2,8,1024]{2,0,1:T(2,128)(2,1)S(1)} %copy.20), channel_id=1, replica_groups=mesh['dp'=4,'mp'=8] {'mp'}, dimensions={1} | all-to-all | bytes 65536 | tf_op jit(solution)/shard_map/all_to_all | solution.py:124
  71.3 13.5 %all_gather.6 = bf16[64,1024]{1,0:T(8,128)(2,1)S(1)} all-gather(bf16[16,1024]{1,0:T(8,128)(2,1)S(1)} %all_to_all.38), channel_id=1, replica_groups=mesh['dp'=4,'mp'=8] {'dp'}, dimensions={0}, use_global_device_ids=true | all-gather | bytes 163840 | tf_op jit(solution)/shard_map/all_gather | solution.py:126
  84.8 3.8 %fusion.62 = f32[64,2048]{1,0:T(8,128)} fusion(bf16[64,1024]{1,0:T(8,128)(2,1)S(1)} %all_gather.6, bf16[1024,2048]{1,0:T(8,128)(2,1)} %param.17), kind=kOutput, calls=%fused_computation.153 | convolution fusion | flops 268435456 | bytes 4849664 | tf_op jit(solution)/shard_map/dot_general | solution.py:125
  88.7 51.1 %all-reduce.5.cloned.1.call-done = f32[64,2048]{1,0:T(8,128)} async-done(((f32[64,2048]{1,0:T(8,128)}), f32[64,2048]{1,0:T(8,128)}) %all-reduce.5.cloned.1.call-update) | async-done | bytes 524304 | tf_op jit(solution)/shard_map/psum | solution.py:130
  139.8 1.3 fusion.18
  141.4 3.0 %fusion.26 = f32[64,1024]{1,0:T(8,128)S(1)} fusion(bf16[2048,1024]{1,0:T(8,128)(2,1)} %param.15, bf16[64,2048]{1,0:T(8,128)(2,1)S(1)} %get-tuple-element.8, f32[2048]{0:T(1024)S(1)} %convert_element_type.90), kind=kOutput, calls=%fused_computation.48 | convolution fusion | flops 268828672 | bytes 4726784 | tf_op jit(solution)/shard_map/dot_general | solution.py:88
  144.5 0.7 pad_maximum_fusion.1
  145.3 11.7 %all-reduce.1 = f32[64]{0:T(128)S(1)} all-reduce(f32[64]{0:T(128)S(1)} %get-tuple-element.6), channel_id=5, replica_groups=mesh['dp'=4,'mp'=8] {'dp'}, use_global_device_ids=true, to_apply=%region_8.11.clone | all-reduce | flops 64 | bytes 512
  157.0 7.7 %reduce-scatter.5.cloned.1.call-done = f32[16,1280]{1,0:T(8,128)} async-done(((f32[64,1280]{1,0:T(8,128)}), f32[16,1280]{1,0:T(8,128)}) %reduce-scatter.5.cloned.1.call-update) | async-done | bytes 81936 | tf_op jit(solution)/shard_map/reduce_scatter | solution.py:93
  164.8 1.0 broadcast_multiply_fusion
  166.3 0.6 constant_dynamic-update-slice_fusion.14
  167.6 0.6 constant_dynamic-update-slice_fusion.12
  170.6 3.7 %all-to-all-start.2 = ((f32[8,2,1280]{2,1,0:T(2,128)}), f32[8,2,1280]{2,1,0:T(2,128)S(1)}, u32[]{:S(2)}, u32[]{:S(2)}) async-start(f32[8,2,1280]{2,1,0:T(2,128)} %constant_dynamic-update-slice_fusion.8), calls=%async_computation.4 | async-start | bytes 163840 | tf_op jit(solution)/shard_map/all_to_all | solution.py:98
  174.2 0.8 scatter_custom_fusion
  175.0 4.3 %all-to-all-done.2 = f32[8,2,1280]{2,1,0:T(2,128)S(1)} async-done(((f32[8,2,1280]{2,1,0:T(2,128)}), f32[8,2,1280]{2,1,0:T(2,128)S(1)}, u32[]{:S(2)}, u32[]{:S(2)}) %all-to-all-start.2) | async-done | bytes 81952 | tf_op jit(solution)/shard_map/all_to_all | solution.py:98
  179.7 2.4 fusion.61
  182.5 2.0 fusion.12
  184.6 0.6 copy.23
  185.2 3.3 %all-to-all-start.3 = ((bf16[2,8,1024]{2,0,1:T(2,128)(2,1)}), bf16[2,8,1024]{2,0,1:T(2,128)(2,1)S(1)}, u32[]{:S(2)}, u32[]{:S(2)}) async-start(bf16[2,8,1024]{2,0,1:T(2,128)(2,1)} %copy.23), calls=%async_computation.5 | async-start | bytes 65536 | tf_op jit(solution)/shard_map/all_to_all | solution.py:124
  188.6 4.7 %all-to-all-done.3 = bf16[2,8,1024]{2,0,1:T(2,128)(2,1)S(1)} async-done(((bf16[2,8,1024]{2,0,1:T(2,128)(2,1)}), bf16[2,8,1024]{2,0,1:T(2,128)(2,1)S(1)}, u32[]{:S(2)}, u32[]{:S(2)}) %all-to-all-start.3) | async-done | bytes 32800 | tf_op jit(solution)/shard_map/all_to_all | solution.py:124
  193.4 13.6 %all_gather.7 = bf16[64,1024]{1,0:T(8,128)(2,1)S(1)} all-gather(bf16[16,1024]{1,0:T(8,128)(2,1)S(1)} %all_to_all.43), channel_id=1, replica_groups=mesh['dp'=4,'mp'=8] {'dp'}, dimensions={0}, use_global_device_ids=true | all-gather | bytes 163840 | tf_op jit(solution)/shard_map/all_gather | solution.py:126
  207.0 3.8 %fusion.63 = f32[64,2048]{1,0:T(8,128)} fusion(bf16[64,1024]{1,0:T(8,128)(2,1)S(1)} %all_gather.7, bf16[1024,2048]{1,0:T(8,128)(2,1)} %param.17), kind=kOutput, calls=%fused_computation.154 | convolution fusion | flops 268435456 | bytes 4849664 | tf_op jit(solution)/shard_map/dot_general | solution.py:125
  210.9 51.1 %all-reduce.7.cloned.1.call-done = f32[64,2048]{1,0:T(8,128)} async-done(((f32[64,2048]{1,0:T(8,128)}), f32[64,2048]{1,0:T(8,128)}) %all-reduce.7.cloned.1.call-update) | async-done | bytes 524304 | tf_op jit(solution)/shard_map/psum | solution.py:130
  262.0 1.1 fusion.19
  263.1 0.7 gather_fusion.3
  263.8 0.8 broadcast_select_fusion
  (77 shorter events, 8.6 us)
Async XLA Ops:
  6.5 5.5 %copy-start = (bf16[2048,256]{1,0:T(8,128)(2,1)S(1)}, bf16[2048,256]{1,0:T(8,128)(2,1)}, u32[]{:S(2)}) copy-start(bf16[2048,256]{1,0:T(8,128)(2,1)} %param.16) | copy-start | bytes 3145732
  6.5 37.6 %reduce-scatter.3.cloned.1.call-start = ((), (), s32[]{:S(2)}) async-start(), calls=%async_computation.6 | async-start | bytes 409600 | tf_op jit(solution)/shard_map/reduce_scatter | solution.py:93
  16.5 19.3 %copy-start.1 = (s32[64]{0:T(128)S(1)}, s32[64]{0:T(128)}, u32[]{:S(2)}) copy-start(s32[64]{0:T(128)} %param.19) | copy-start | bytes 772
  16.5 20.1 %copy-start.2 = (u32[32]{0:T(128)S(1)}, u32[32]{0:T(128)}, u32[]{:S(2)}) copy-start(u32[32]{0:T(128)} %constant.56) | copy-start | bytes 388
  50.0 8.8 %all-to-all-start = ((f32[8,2,1280]{2,1,0:T(2,128)}), f32[8,2,1280]{2,1,0:T(2,128)S(1)}, u32[]{:S(2)}, u32[]{:S(2)}) async-start(f32[8,2,1280]{2,1,0:T(2,128)} %constant_dynamic-update-slice_fusion), calls=%async_computation.1 | async-start | bytes 163840 | tf_op jit(solution)/shard_map/all_to_all | solution.py:98
  53.7 86.2 %all-reduce.5.cloned.1.call-start = ((), (), s32[]{:S(2)}) async-start(), calls=%async_computation.7 | async-start | bytes 1048576 | tf_op jit(solution)/shard_map/psum | solution.py:130
  88.7 76.1 %reduce-scatter.5.cloned.1.call-start = ((), (), s32[]{:S(2)}) async-start(), calls=%async_computation.8 | async-start | bytes 409600 | tf_op jit(solution)/shard_map/reduce_scatter | solution.py:93
  170.6 8.8 %all-to-all-start.2 = ((f32[8,2,1280]{2,1,0:T(2,128)}), f32[8,2,1280]{2,1,0:T(2,128)S(1)}, u32[]{:S(2)}, u32[]{:S(2)}) async-start(f32[8,2,1280]{2,1,0:T(2,128)} %constant_dynamic-update-slice_fusion.8), calls=%async_computation.4 | async-start | bytes 163840 | tf_op jit(solution)/shard_map/all_to_all | solution.py:98
  185.2 8.1 %all-to-all-start.3 = ((bf16[2,8,1024]{2,0,1:T(2,128)(2,1)}), bf16[2,8,1024]{2,0,1:T(2,128)(2,1)S(1)}, u32[]{:S(2)}, u32[]{:S(2)}) async-start(bf16[2,8,1024]{2,0,1:T(2,128)(2,1)} %copy.23), calls=%async_computation.5 | async-start | bytes 65536 | tf_op jit(solution)/shard_map/all_to_all | solution.py:124
  188.6 73.4 %all-reduce.7.cloned.1.call-start = ((), (), s32[]{:S(2)}) async-start(), calls=%async_computation.9 | async-start | bytes 1048576 | tf_op jit(solution)/shard_map/psum | solution.py:130
Sparse Core Ops, SparseCore 0:
  16.4 22.8 reduce-scatter.2
  88.8 50.9 all-reduce.4
  145.4 19.3 reduce-scatter.4
  211.0 50.9 all-reduce.6
